TPU v7x, 32 devices: a whole 2x2x4 slice. The times are simulated.
32 devices in a mesh: row: 8 (over z, core), col: 4 (over y, x).
Axes of the slice: x: 2, y: 2, z: 4, core: 2. Of those that a mesh axis runs over, the one named last changes fastest.
Arguments:
- running_cost: float32 [2048, 2048], P('row', 'col'), may hold values from 0.5 to 7.5, as said below
- control_x: float32 [2048, 2048], P('row', 'col'), may hold values from -6 to 6
- control_y: float32 [2048, 2048], P('row', 'col'), may hold values from -6 to 6
- prior_density: float32 [2048, 2048], P('row', 'col'), may hold values from 0.5 to 2
Outputs:
- value_field: float32 [2048, 2048], P('row', 'col')
- density: float32 [2048, 2048], P('row', 'col')
- ergodic: float32 [], replicated
Inputs may be any that keep to these rules, and one draw needn't show every extreme that they name: `running_cost`: strictly positive.
All inputs are finite; a program needn't handle non-finite values.
Results may differ from a plain program's by a relative error of at most 0.0003.
Values sent between devices are 32-bit elements; how exact they have to be, the bound alone decides.
No kernel may reach another device: no remote copies, remote signals or barrier semaphores. Data moves between devices by JAX's collectives and lax.ppermute only.
A program may use at most 64 MiB of HBM per device.

v0:
```python
import jax
import jax.numpy as jnp
from jax import lax
from jax.sharding import PartitionSpec as P

ITERS = 3
discount_rate = 0.05
diffusion = 0.25


def padded_2(cells, sides, width):
    for axis, dim in sides:
        count = lax.axis_size(axis)
        ends = count - 1
        head = lax.slice_in_dim(cells, 0, width, axis=dim)
        tail = lax.slice_in_dim(cells, cells.shape[dim] - width, cells.shape[dim], axis=dim)
        cells = jnp.concatenate(
            [
                lax.ppermute(tail, axis, [(i, (i + 1) % count) for i in range(ends)]),
                cells,
                lax.ppermute(head, axis, [((i + 1) % count, i) for i in range(ends)]),
            ],
            axis=dim,
        )
    return cells


def interior(padded):
    return padded[1:-1, 1:-1]


def neighbours(padded):
    return (padded[2:, 1:-1], padded[:-2, 1:-1], padded[1:-1, 2:], padded[1:-1, :-2])


def coefficients(conduct, padded_conduct, zeroth):
    weights = tuple(
        (diffusion * 0.5 * (conduct + outside) for outside in neighbours(padded_conduct))
    )
    center = zeroth + (weights[0] + weights[1] + (weights[2] + weights[3]))
    return (center,) + weights


def operator_apply(padded, coeffs):
    beside = neighbours(padded)
    inflow = (
        coeffs[1] * beside[0]
        + coeffs[2] * beside[1]
        + (coeffs[3] * beside[2] + coeffs[4] * beside[3])
    )
    return coeffs[0] * interior(padded) - inflow


def operate(source, coeffs):
    padded = padded_2(source, (("row", 0), ("col", 1)), 1)
    return (padded, operator_apply(padded, coeffs))


def products(residual, applied):
    return lax.psum((jnp.sum(residual * residual), jnp.sum(residual * applied)), ("row", "col"))


def conjugate(coeffs, forcing):
    solution = jnp.zeros_like(forcing)
    padded_solution = jnp.zeros((forcing.shape[0] + 2, forcing.shape[1] + 2), jnp.float32)
    residual = forcing
    padded_res, applied = operate(residual, coeffs)
    norm_now, product = products(residual, applied)
    step_size = norm_now / product
    direction, image_dir, padded_dir = (residual, applied, padded_res)
    for iteration in range(ITERS):
        solution = solution + step_size * direction
        if iteration + 1 < ITERS:
            residual = residual - step_size * image_dir
            padded_res, applied = operate(residual, coeffs)
            norm_next, product = products(residual, applied)
            beta_ratio = norm_next / norm_now
            step_size = norm_next / (product - beta_ratio * norm_next / step_size)
            direction = residual + beta_ratio * direction
            image_dir = applied + beta_ratio * image_dir
            norm_now = norm_next
    return (solution, padded_solution)


def body(running_cost, control_x, control_y, prior_density):
    control_cost = 0.5 * (control_x * control_x + control_y * control_y)
    conduct = 1.0 + control_cost
    forcing = running_cost + control_cost
    padded_conduct = padded_2(conduct, (("row", 0), ("col", 1)), 1)
    bellman = coefficients(conduct, padded_conduct, discount_rate)
    value_field, padded_solution = conjugate(bellman, forcing)
    padded_value = padded_2(value_field, (("row", 0), ("col", 1)), 1)
    beside = neighbours(padded_value)
    slope_row = 0.5 * (beside[0] - beside[1])
    slope_col = 0.5 * (beside[2] - beside[3])
    congestion = (slope_row * slope_row + slope_col * slope_col) / (2.0 * diffusion)
    planck = coefficients(conduct, padded_conduct, discount_rate + congestion)
    weighted = jnp.sum(prior_density * (forcing - discount_rate * value_field))
    weight_total = jnp.sum(prior_density)
    density, unused = conjugate(planck, prior_density)
    totals = lax.psum((weighted, weight_total), ("row", "col"))
    ergodic = totals[0] / totals[1]
    return (value_field, density, ergodic)


def solution(mesh):
    in_specs = (P("row", "col"), P("row", "col"), P("row", "col"), P("row", "col"))
    out_specs = (P("row", "col"), P("row", "col"), P())
    return jax.shard_map(body, mesh=mesh, in_specs=in_specs, out_specs=out_specs, check_vma=False)
```

profile of v0, /device:TPU:0, one launch (start us, length us, event | category | flops | bytes accessed | tf_op | source)
XLA Modules:
  0.0 410.6 jit_solution(13232752948674389063)
XLA Ops:
  0.6 1.5 broadcast_add_fusion
  2.2 2.4 collective-permute-start.5
  4.6 1.3 collective-permute-start.4
  5.9 5.2 %collective-permute-start.1 = (f32[1,512]{1,0:T(1,128)S(1)}, f32[1,512]{1,0:T(1,128)S(1)}, u32[]{:S(2)}, u32[]{:S(2)}) collective-permute-start(f32[1,512]{1,0:T(1,128)S(1)} %get-tuple-element.65), channel_id=1, source_target_pairs={{0,4},{4,8},{8,12},{12,16},{16,20},{20,24},{24,28},{1,5},{5,9},{9,... | collective-permute-start | bytes 6152 | tf_op jit(solution)/shard_map/ppermute | solution.py:19
  11.1 1.3 collective-permute-start
  12.5 1.3 collective-permute-start.6
  13.8 4.6 %collective-permute-start.7 = (f32[258,1]{1,0:T(8,128)S(1)}, f32[258,1]{1,0:T(8,128)S(1)}, u32[]{:S(2)}, u32[]{:S(2)}) collective-permute-start(f32[258,1]{1,0:T(8,128)S(1)} %get-tuple-element.52), channel_id=1, source_target_pairs={{0,1},{1,2},{2,3},{4,5},{5,6},{6,7},{8,9},{9,10},{10,11},{12,13},{... | collective-permute-start | bytes 3104 | tf_op jit(solution)/shard_map/ppermute | solution.py:19
  18.6 1.3 collective-permute-start.2
  19.9 4.9 %collective-permute-start.3 = (f32[258,1]{1,0:T(8,128)S(1)}, f32[258,1]{1,0:T(8,128)S(1)}, u32[]{:S(2)}, u32[]{:S(2)}) collective-permute-start(f32[258,1]{1,0:T(8,128)S(1)} %get-tuple-element.50), channel_id=1, source_target_pairs={{0,1},{1,2},{2,3},{4,5},{5,6},{6,7},{8,9},{9,10},{10,11},{12,13},{... | collective-permute-start | bytes 3104 | tf_op jit(solution)/shard_map/ppermute | solution.py:19
  24.8 2.5 collective-permute-done.2
  27.9 1.4 multiply_reduce_fusion.9
  29.3 44.4 %all-reduce.5 = (f32[]{:T(128)}, f32[]{:T(128)}) all-reduce(f32[]{:T(128)} %get-tuple-element.12, f32[]{:T(128)} %get-tuple-element.11), channel_id=1, replica_groups=mesh['row'=8,'col'=4] {'row','col'}, use_global_device_ids=true, to_apply=%region_1.0 | all-reduce | flops 2 | bytes 16 | tf_op jit(solution)/shard_map/psum | solution.py:60
  76.5 1.3 collective-permute-start.8
  77.8 3.4 collective-permute-done.8
  81.4 1.3 collective-permute-start.10
  82.7 4.8 %collective-permute-start.11 = (f32[258,1]{1,0:T(8,128)S(1)}, f32[258,1]{1,0:T(8,128)S(1)}, u32[]{:S(2)}, u32[]{:S(2)}) collective-permute-start(f32[258,1]{1,0:T(8,128)S(1)} %get-tuple-element.48), channel_id=1, source_target_pairs={{0,1},{1,2},{2,3},{4,5},{5,6},{6,7},{8,9},{9,10},{10,11},{12,13},{... | collective-permute-start | bytes 3104 | tf_op jit(solution)/shard_map/ppermute | solution.py:19
  88.5 1.5 collective-permute-done.11
  90.0 1.4 multiply_reduce_fusion.7
  91.4 44.4 %all-reduce.4 = (f32[]{:T(128)}, f32[]{:T(128)}) all-reduce(f32[]{:T(128)} %get-tuple-element.10, f32[]{:T(128)} %get-tuple-element.9), channel_id=1, replica_groups=mesh['row'=8,'col'=4] {'row','col'}, use_global_device_ids=true, to_apply=%region_5.0 | all-reduce | flops 2 | bytes 16 | tf_op jit(solution)/shard_map/psum | solution.py:60
  141.0 1.4 collective-permute-start.13
  142.4 1.3 collective-permute-start.12
  143.7 1.9 collective-permute-done.12
  145.7 1.3 collective-permute-start.14
  147.0 4.8 %collective-permute-start.15 = (f32[258,1]{1,0:T(8,128)S(1)}, f32[258,1]{1,0:T(8,128)S(1)}, u32[]{:S(2)}, u32[]{:S(2)}) collective-permute-start(f32[258,1]{1,0:T(8,128)S(1)} %get-tuple-element.46), channel_id=1, source_target_pairs={{0,1},{1,2},{2,3},{4,5},{5,6},{6,7},{8,9},{9,10},{10,11},{12,13},{... | collective-permute-start | bytes 3104 | tf_op jit(solution)/shard_map/ppermute | solution.py:19
  151.9 3.9 collective-permute-start.21
  155.8 1.3 collective-permute-start.20
  157.2 1.4 fusion.41
  158.6 41.7 %all-reduce.3 = (f32[]{:T(128)}, f32[]{:T(128)}) all-reduce(f32[]{:T(128)} %get-tuple-element.31, f32[]{:T(128)} %fusion.41), channel_id=1, replica_groups=mesh['row'=8,'col'=4] {'row','col'}, use_global_device_ids=true, to_apply=%region_9.0 | all-reduce | flops 2 | bytes 16 | tf_op jit(solution)/shard_map/psum | solution.py:60
  205.6 1.3 collective-permute-start.16
  208.8 5.0 %collective-permute-start.23 = (f32[258,1]{1,0:T(8,128)S(1)}, f32[258,1]{1,0:T(8,128)S(1)}, u32[]{:S(2)}, u32[]{:S(2)}) collective-permute-start(f32[258,1]{1,0:T(8,128)S(1)} %get-tuple-element.44), channel_id=1, source_target_pairs={{0,1},{1,2},{2,3},{4,5},{5,6},{6,7},{8,9},{9,10},{10,11},{12,13},{... | collective-permute-start | bytes 3104 | tf_op jit(solution)/shard_map/ppermute | solution.py:19
  214.0 1.3 collective-permute-start.18
  215.3 5.4 %collective-permute-start.19 = (f32[258,1]{1,0:T(8,128)S(1)}, f32[258,1]{1,0:T(8,128)S(1)}, u32[]{:S(2)}, u32[]{:S(2)}) collective-permute-start(f32[258,1]{1,0:T(8,128)S(1)} %get-tuple-element.42), channel_id=1, source_target_pairs={{0,1},{1,2},{2,3},{4,5},{5,6},{6,7},{8,9},{9,10},{10,11},{12,13},{... | collective-permute-start | bytes 3104 | tf_op jit(solution)/shard_map/ppermute | solution.py:19
  220.8 2.5 collective-permute-done.18
  223.6 3.4 fusion.71
  227.0 44.8 %all-reduce.2 = (f32[]{:T(128)}, f32[]{:T(128)}) all-reduce(f32[]{:T(128)} %get-tuple-element.5, f32[]{:T(128)} %get-tuple-element.4), channel_id=1, replica_groups=mesh['row'=8,'col'=4] {'row','col'}, use_global_device_ids=true, to_apply=%region_13.0 | all-reduce | flops 2 | bytes 16 | tf_op jit(solution)/shard_map/psum | solution.py:60
  274.5 1.3 collective-permute-start.24
  275.9 2.3 collective-permute-done.24
  279.6 4.8 %collective-permute-start.27 = (f32[258,1]{1,0:T(8,128)S(1)}, f32[258,1]{1,0:T(8,128)S(1)}, u32[]{:S(2)}, u32[]{:S(2)}) collective-permute-start(f32[258,1]{1,0:T(8,128)S(1)} %get-tuple-element.40), channel_id=1, source_target_pairs={{0,1},{1,2},{2,3},{4,5},{5,6},{6,7},{8,9},{9,10},{10,11},{12,13},{... | collective-permute-start | bytes 3104 | tf_op jit(solution)/shard_map/ppermute | solution.py:19
  285.5 1.5 collective-permute-done.27
  287.0 3.9 multiply_reduce_fusion.2
  290.9 44.6 %all-reduce.1 = (f32[]{:T(128)}, f32[]{:T(128)}) all-reduce(f32[]{:T(128)} %get-tuple-element.8, f32[]{:T(128)} %get-tuple-element.7), channel_id=1, replica_groups=mesh['row'=8,'col'=4] {'row','col'}, use_global_device_ids=true, to_apply=%region_17.0 | all-reduce | flops 2 | bytes 16 | tf_op jit(solution)/shard_map/psum | solution.py:60
  339.9 1.8 multiply_reduce_fusion.1
  343.1 1.4 collective-permute-start.28
  344.5 2.4 collective-permute-done.28
  348.3 4.8 %collective-permute-start.31 = (f32[258,1]{1,0:T(8,128)S(1)}, f32[258,1]{1,0:T(8,128)S(1)}, u32[]{:S(2)}, u32[]{:S(2)}) collective-permute-start(f32[258,1]{1,0:T(8,128)S(1)} %get-tuple-element.38), channel_id=1, source_target_pairs={{0,1},{1,2},{2,3},{4,5},{5,6},{6,7},{8,9},{9,10},{10,11},{12,13},{... | collective-permute-start | bytes 3104 | tf_op jit(solution)/shard_map/ppermute | solution.py:19
  354.2 1.5 collective-permute-done.31
  355.7 3.1 fusion.5
  358.8 44.5 %all-reduce = (f32[]{:T(128)}, f32[]{:T(128)}, f32[]{:T(128)}, f32[]{:T(128)}) all-reduce(f32[]{:T(128)} %get-tuple-element.27, f32[]{:T(128)} %fusion.5, f32[]{:T(128)} %get-tuple-element.6, f32[]{:T(128)} %get-tuple-element.3), channel_id=1, replica_groups=mesh['row'=8,'col'=4] {'row','col'}, use_global_device_ids=true, to_apply=%region_21.0 | all-reduce | flops 4 | bytes 32 | tf_op jit(solution)/shard_map/psum | solution.py:60
  (81 shorter events, 16.7 us)
Async XLA Ops:
  2.2 10.2 %collective-permute-start.5 = (f32[1,512]{1,0:T(1,128)S(1)}, f32[1,512]{1,0:T(1,128)S(1)}, u32[]{:S(2)}, u32[]{:S(2)}) collective-permute-start(f32[1,512]{1,0:T(1,128)S(1)} %get-tuple-element.67), channel_id=1, source_target_pairs={{0,4},{4,8},{8,12},{12,16},{16,20},{20,24},{24,28},{1,5},{5,9},{9,... | collective-permute-start | bytes 6152 | tf_op jit(solution)/shard_map/ppermute | solution.py:19
  4.6 7.8 %collective-permute-start.4 = (f32[1,512]{1,0:T(1,128)S(1)}, f32[1,512]{1,0:T(1,128)S(1)}, u32[]{:S(2)}, u32[]{:S(2)}) collective-permute-start(f32[1,512]{1,0:T(1,128)S(1)} %get-tuple-element.68), channel_id=1, source_target_pairs={{4,0},{8,4},{12,8},{16,12},{20,16},{24,20},{28,24},{5,1},{9,5},{13... | collective-permute-start | bytes 6152 | tf_op jit(solution)/shard_map/ppermute | solution.py:21
  5.9 12.5 %collective-permute-start.1 = (f32[1,512]{1,0:T(1,128)S(1)}, f32[1,512]{1,0:T(1,128)S(1)}, u32[]{:S(2)}, u32[]{:S(2)}) collective-permute-start(f32[1,512]{1,0:T(1,128)S(1)} %get-tuple-element.65), channel_id=1, source_target_pairs={{0,4},{4,8},{8,12},{12,16},{16,20},{20,24},{24,28},{1,5},{5,9},{9,... | collective-permute-start | bytes 6152 | tf_op jit(solution)/shard_map/ppermute | solution.py:19
  11.1 7.3 %collective-permute-start = (f32[1,512]{1,0:T(1,128)S(1)}, f32[1,512]{1,0:T(1,128)S(1)}, u32[]{:S(2)}, u32[]{:S(2)}) collective-permute-start(f32[1,512]{1,0:T(1,128)S(1)} %get-tuple-element.66), channel_id=1, source_target_pairs={{4,0},{8,4},{12,8},{16,12},{20,16},{24,20},{28,24},{5,1},{9,5},{13... | collective-permute-start | bytes 6152 | tf_op jit(solution)/shard_map/ppermute | solution.py:21
  12.5 12.2 %collective-permute-start.6 = (f32[258,1]{1,0:T(8,128)S(1)}, f32[258,1]{1,0:T(8,128)S(1)}, u32[]{:S(2)}, u32[]{:S(2)}) collective-permute-start(f32[258,1]{1,0:T(8,128)S(1)} %get-tuple-element.51), channel_id=1, source_target_pairs={{1,0},{2,1},{3,2},{5,4},{6,5},{7,6},{9,8},{10,9},{11,10},{13,12},{... | collective-permute-start | bytes 3104 | tf_op jit(solution)/shard_map/ppermute | solution.py:21
  13.8 11.0 %collective-permute-start.7 = (f32[258,1]{1,0:T(8,128)S(1)}, f32[258,1]{1,0:T(8,128)S(1)}, u32[]{:S(2)}, u32[]{:S(2)}) collective-permute-start(f32[258,1]{1,0:T(8,128)S(1)} %get-tuple-element.52), channel_id=1, source_target_pairs={{0,1},{1,2},{2,3},{4,5},{5,6},{6,7},{8,9},{9,10},{10,11},{12,13},{... | collective-permute-start | bytes 3104 | tf_op jit(solution)/shard_map/ppermute | solution.py:19
  18.4 138.7 %copy-start.4 = (f32[1,512]{1,0:T(1,128)}, f32[1,512]{1,0:T(1,128)S(1)}, u32[]{:S(2)}) copy-start(f32[1,512]{1,0:T(1,128)S(1)} %collective-permute-done) | copy-start | bytes 6148
  18.6 8.7 %collective-permute-start.2 = (f32[258,1]{1,0:T(8,128)S(1)}, f32[258,1]{1,0:T(8,128)S(1)}, u32[]{:S(2)}, u32[]{:S(2)}) collective-permute-start(f32[258,1]{1,0:T(8,128)S(1)} %get-tuple-element.49), channel_id=1, source_target_pairs={{1,0},{2,1},{3,2},{5,4},{6,5},{7,6},{9,8},{10,9},{11,10},{13,12},{... | collective-permute-start | bytes 3104 | tf_op jit(solution)/shard_map/ppermute | solution.py:21
  19.9 8.0 %collective-permute-start.3 = (f32[258,1]{1,0:T(8,128)S(1)}, f32[258,1]{1,0:T(8,128)S(1)}, u32[]{:S(2)}, u32[]{:S(2)}) collective-permute-start(f32[258,1]{1,0:T(8,128)S(1)} %get-tuple-element.50), channel_id=1, source_target_pairs={{0,1},{1,2},{2,3},{4,5},{5,6},{6,7},{8,9},{9,10},{10,11},{12,13},{... | collective-permute-start | bytes 3104 | tf_op jit(solution)/shard_map/ppermute | solution.py:19
  75.2 2.6 collective-permute-start.9
  76.5 4.7 %collective-permute-start.8 = (f32[1,512]{1,0:T(1,128)S(1)}, f32[1,512]{1,0:T(1,128)S(1)}, u32[]{:S(2)}, u32[]{:S(2)}) collective-permute-start(f32[1,512]{1,0:T(1,128)S(1)} %get-tuple-element.64), channel_id=1, source_target_pairs={{4,0},{8,4},{12,8},{16,12},{20,16},{24,20},{28,24},{5,1},{9,5},{13... | collective-permute-start | bytes 6152 | tf_op jit(solution)/shard_map/ppermute | solution.py:21
  81.4 7.2 %collective-permute-start.10 = (f32[258,1]{1,0:T(8,128)S(1)}, f32[258,1]{1,0:T(8,128)S(1)}, u32[]{:S(2)}, u32[]{:S(2)}) collective-permute-start(f32[258,1]{1,0:T(8,128)S(1)} %get-tuple-element.47), channel_id=1, source_target_pairs={{1,0},{2,1},{3,2},{5,4},{6,5},{7,6},{9,8},{10,9},{11,10},{13,12},{... | collective-permute-start | bytes 3104 | tf_op jit(solution)/shard_map/ppermute | solution.py:21
  82.7 7.4 %collective-permute-start.11 = (f32[258,1]{1,0:T(8,128)S(1)}, f32[258,1]{1,0:T(8,128)S(1)}, u32[]{:S(2)}, u32[]{:S(2)}) collective-permute-start(f32[258,1]{1,0:T(8,128)S(1)} %get-tuple-element.48), channel_id=1, source_target_pairs={{0,1},{1,2},{2,3},{4,5},{5,6},{6,7},{8,9},{9,10},{10,11},{12,13},{... | collective-permute-start | bytes 3104 | tf_op jit(solution)/shard_map/ppermute | solution.py:19
  140.9 10.9 %copy-start.1 = (f32[256,512]{1,0:T(8,128)S(1)}, f32[256,512]{1,0:T(8,128)}, u32[]{:S(2)}) copy-start(f32[256,512]{1,0:T(8,128)} %param.7) | copy-start | bytes 1572868
  141.0 2.7 collective-permute-start.13
  142.4 3.2 collective-permute-start.12
  145.7 11.4 %collective-permute-start.14 = (f32[258,1]{1,0:T(8,128)S(1)}, f32[258,1]{1,0:T(8,128)S(1)}, u32[]{:S(2)}, u32[]{:S(2)}) collective-permute-start(f32[258,1]{1,0:T(8,128)S(1)} %get-tuple-element.45), channel_id=1, source_target_pairs={{1,0},{2,1},{3,2},{5,4},{6,5},{7,6},{9,8},{10,9},{11,10},{13,12},{... | collective-permute-start | bytes 3104 | tf_op jit(solution)/shard_map/ppermute | solution.py:21
  147.0 10.1 %collective-permute-start.15 = (f32[258,1]{1,0:T(8,128)S(1)}, f32[258,1]{1,0:T(8,128)S(1)}, u32[]{:S(2)}, u32[]{:S(2)}) collective-permute-start(f32[258,1]{1,0:T(8,128)S(1)} %get-tuple-element.46), channel_id=1, source_target_pairs={{0,1},{1,2},{2,3},{4,5},{5,6},{6,7},{8,9},{9,10},{10,11},{12,13},{... | collective-permute-start | bytes 3104 | tf_op jit(solution)/shard_map/ppermute | solution.py:19
  151.9 55.0 %collective-permute-start.21 = (f32[1,512]{1,0:T(1,128)S(1)}, f32[1,512]{1,0:T(1,128)S(1)}, u32[]{:S(2)}, u32[]{:S(2)}) collective-permute-start(f32[1,512]{1,0:T(1,128)S(1)} %get-tuple-element.59), channel_id=1, source_target_pairs={{0,4},{4,8},{8,12},{12,16},{16,20},{20,24},{24,28},{1,5},{5,9},{9,... | collective-permute-start | bytes 6152 | tf_op jit(solution)/shard_map/ppermute | solution.py:19
  155.8 51.1 %collective-permute-start.20 = (f32[1,512]{1,0:T(1,128)S(1)}, f32[1,512]{1,0:T(1,128)S(1)}, u32[]{:S(2)}, u32[]{:S(2)}) collective-permute-start(f32[1,512]{1,0:T(1,128)S(1)} %get-tuple-element.60), channel_id=1, source_target_pairs={{4,0},{8,4},{12,8},{16,12},{20,16},{24,20},{28,24},{5,1},{9,5},{13... | collective-permute-start | bytes 6152 | tf_op jit(solution)/shard_map/ppermute | solution.py:21
  204.2 151.4 %copy-start = (f32[256,512]{1,0:T(8,128)}, f32[256,512]{1,0:T(8,128)S(1)}, u32[]{:S(2)}) copy-start(f32[256,512]{1,0:T(8,128)S(1)} %multiply_add_fusion.1) | copy-start | bytes 1572868
  204.3 9.6 %collective-permute-start.17 = (f32[1,512]{1,0:T(1,128)S(1)}, f32[1,512]{1,0:T(1,128)S(1)}, u32[]{:S(2)}, u32[]{:S(2)}) collective-permute-start(f32[1,512]{1,0:T(1,128)S(1)} %get-tuple-element.57), channel_id=1, source_target_pairs={{0,4},{4,8},{8,12},{12,16},{16,20},{20,24},{24,28},{1,5},{5,9},{9,... | collective-permute-start | bytes 6152 | tf_op jit(solution)/shard_map/ppermute | solution.py:19
  205.6 8.3 %collective-permute-start.16 = (f32[1,512]{1,0:T(1,128)S(1)}, f32[1,512]{1,0:T(1,128)S(1)}, u32[]{:S(2)}, u32[]{:S(2)}) collective-permute-start(f32[1,512]{1,0:T(1,128)S(1)} %get-tuple-element.58), channel_id=1, source_target_pairs={{4,0},{8,4},{12,8},{16,12},{20,16},{24,20},{28,24},{5,1},{9,5},{13... | collective-permute-start | bytes 6152 | tf_op jit(solution)/shard_map/ppermute | solution.py:21
  206.9 0.6 copy-start.11
  206.9 0.6 copy-start.13
  207.5 13.3 %collective-permute-start.22 = (f32[258,1]{1,0:T(8,128)S(1)}, f32[258,1]{1,0:T(8,128)S(1)}, u32[]{:S(2)}, u32[]{:S(2)}) collective-permute-start(f32[258,1]{1,0:T(8,128)S(1)} %get-tuple-element.43), channel_id=1, source_target_pairs={{1,0},{2,1},{3,2},{5,4},{6,5},{7,6},{9,8},{10,9},{11,10},{13,12},{... | collective-permute-start | bytes 3104 | tf_op jit(solution)/shard_map/ppermute | solution.py:21
  208.8 12.0 %collective-permute-start.23 = (f32[258,1]{1,0:T(8,128)S(1)}, f32[258,1]{1,0:T(8,128)S(1)}, u32[]{:S(2)}, u32[]{:S(2)}) collective-permute-start(f32[258,1]{1,0:T(8,128)S(1)} %get-tuple-element.44), channel_id=1, source_target_pairs={{0,1},{1,2},{2,3},{4,5},{5,6},{6,7},{8,9},{9,10},{10,11},{12,13},{... | collective-permute-start | bytes 3104 | tf_op jit(solution)/shard_map/ppermute | solution.py:19
  213.8 73.1 %copy-start.7 = (f32[1,512]{1,0:T(1,128)}, f32[1,512]{1,0:T(1,128)S(1)}, u32[]{:S(2)}) copy-start(f32[1,512]{1,0:T(1,128)S(1)} %collective-permute-done.17) | copy-start | bytes 6148
  213.9 73.1 %copy-start.9 = (f32[1,512]{1,0:T(1,128)}, f32[1,512]{1,0:T(1,128)S(1)}, u32[]{:S(2)}) copy-start(f32[1,512]{1,0:T(1,128)S(1)} %collective-permute-done.16) | copy-start | bytes 6148
  213.9 9.7 %copy-start.12 = (f32[1,512]{1,0:T(1,128)S(1)}, f32[1,512]{1,0:T(1,128)}, u32[]{:S(2)}) copy-start(f32[1,512]{1,0:T(1,128)} %copy-done.11) | copy-start | bytes 6148
  213.9 9.7 %copy-start.14 = (f32[1,512]{1,0:T(1,128)S(1)}, f32[1,512]{1,0:T(1,128)}, u32[]{:S(2)}) copy-start(f32[1,512]{1,0:T(1,128)} %copy-done.13) | copy-start | bytes 6148
  214.0 9.6 %copy-start.5 = (f32[1,512]{1,0:T(1,128)S(1)}, f32[1,512]{1,0:T(1,128)}, u32[]{:S(2)}) copy-start(f32[1,512]{1,0:T(1,128)} %copy-done.4) | copy-start | bytes 6148
  214.0 9.2 %collective-permute-start.18 = (f32[258,1]{1,0:T(8,128)S(1)}, f32[258,1]{1,0:T(8,128)S(1)}, u32[]{:S(2)}, u32[]{:S(2)}) collective-permute-start(f32[258,1]{1,0:T(8,128)S(1)} %get-tuple-element.41), channel_id=1, source_target_pairs={{1,0},{2,1},{3,2},{5,4},{6,5},{7,6},{9,8},{10,9},{11,10},{13,12},{... | collective-permute-start | bytes 3104 | tf_op jit(solution)/shard_map/ppermute | solution.py:21
  215.3 8.2 %collective-permute-start.19 = (f32[258,1]{1,0:T(8,128)S(1)}, f32[258,1]{1,0:T(8,128)S(1)}, u32[]{:S(2)}, u32[]{:S(2)}) collective-permute-start(f32[258,1]{1,0:T(8,128)S(1)} %get-tuple-element.42), channel_id=1, source_target_pairs={{0,1},{1,2},{2,3},{4,5},{5,6},{6,7},{8,9},{9,10},{10,11},{12,13},{... | collective-permute-start | bytes 3104 | tf_op jit(solution)/shard_map/ppermute | solution.py:19
  223.6 63.4 %copy-start.2 = (f32[258,1]{1,0:T(8,128)}, f32[258,1]{1,0:T(8,128)S(1)}, u32[]{:S(2)}) copy-start(f32[258,1]{1,0:T(8,128)S(1)} %collective-permute-done.19) | copy-start | bytes 3100
  273.2 2.6 collective-permute-start.25
  274.5 3.7 collective-permute-start.24
  278.3 7.2 %collective-permute-start.26 = (f32[258,1]{1,0:T(8,128)S(1)}, f32[258,1]{1,0:T(8,128)S(1)}, u32[]{:S(2)}, u32[]{:S(2)}) collective-permute-start(f32[258,1]{1,0:T(8,128)S(1)} %get-tuple-element.39), channel_id=1, source_target_pairs={{1,0},{2,1},{3,2},{5,4},{6,5},{7,6},{9,8},{10,9},{11,10},{13,12},{... | collective-permute-start | bytes 3104 | tf_op jit(solution)/shard_map/ppermute | solution.py:21
  279.6 7.4 %collective-permute-start.27 = (f32[258,1]{1,0:T(8,128)S(1)}, f32[258,1]{1,0:T(8,128)S(1)}, u32[]{:S(2)}, u32[]{:S(2)}) collective-permute-start(f32[258,1]{1,0:T(8,128)S(1)} %get-tuple-element.40), channel_id=1, source_target_pairs={{0,1},{1,2},{2,3},{4,5},{5,6},{6,7},{8,9},{9,10},{10,11},{12,13},{... | collective-permute-start | bytes 3104 | tf_op jit(solution)/shard_map/ppermute | solution.py:19
  341.8 2.7 collective-permute-start.29
  343.1 12.6 %copy-start.3 = (f32[258,1]{1,0:T(8,128)S(1)}, f32[258,1]{1,0:T(8,128)}, u32[]{:S(2)}) copy-start(f32[258,1]{1,0:T(8,128)} %copy-done.2) | copy-start | bytes 3100
  343.1 3.8 collective-permute-start.28
  346.9 8.8 %copy-start.8 = (f32[1,512]{1,0:T(1,128)S(1)}, f32[1,512]{1,0:T(1,128)}, u32[]{:S(2)}) copy-start(f32[1,512]{1,0:T(1,128)} %copy-done.7) | copy-start | bytes 6148
  346.9 8.8 %copy-start.10 = (f32[1,512]{1,0:T(1,128)S(1)}, f32[1,512]{1,0:T(1,128)}, u32[]{:S(2)}) copy-start(f32[1,512]{1,0:T(1,128)} %copy-done.9) | copy-start | bytes 6148
  347.0 8.7 %copy-start.6 = (f32[1,512]{1,0:T(1,128)S(1)}, f32[1,512]{1,0:T(1,128)}, u32[]{:S(2)}) copy-start(f32[1,512]{1,0:T(1,128)} %copy-done.4) | copy-start | bytes 6148
  347.0 7.2 %collective-permute-start.30 = (f32[258,1]{1,0:T(8,128)S(1)}, f32[258,1]{1,0:T(8,128)S(1)}, u32[]{:S(2)}, u32[]{:S(2)}) collective-permute-start(f32[258,1]{1,0:T(8,128)S(1)} %get-tuple-element.37), channel_id=1, source_target_pairs={{1,0},{2,1},{3,2},{5,4},{6,5},{7,6},{9,8},{10,9},{11,10},{13,12},{... | collective-permute-start | bytes 3104 | tf_op jit(solution)/shard_map/ppermute | solution.py:21
  348.3 7.4 %collective-permute-start.31 = (f32[258,1]{1,0:T(8,128)S(1)}, f32[258,1]{1,0:T(8,128)S(1)}, u32[]{:S(2)}, u32[]{:S(2)}) collective-permute-start(f32[258,1]{1,0:T(8,128)S(1)} %get-tuple-element.38), channel_id=1, source_target_pairs={{0,1},{1,2},{2,3},{4,5},{5,6},{6,7},{8,9},{9,10},{10,11},{12,13},{... | collective-permute-start | bytes 3104 | tf_op jit(solution)/shard_map/ppermute | solution.py:19
where the time goes:
time: 413 us; the launch traced here: 411 us
  blocking collectives  264 us (64%)
  starting transfers between devices  78.2 us (19%)
  waiting for transfers between devices  23.6 us (6%)
  between operations  22.8 us (6%)
  other arithmetic  21 us (5%)
    psum x6, blocking collectives, products(): lax.psum((jnp.sum(residual * residual), jnp.sum(residual * applied)), ('r...  264 us
    ppermute x16, starting transfers between devices, padded_2(): lax.ppermute(tail, axis, [(i, (i + 1) % count) for i in range(ends)])  57.4 us
    ppermute x16, starting transfers between devices, padded_2(): lax.ppermute(head, axis, [((i + 1) % count, i) for i in range(ends)])  20.8 us
    ppermute x16, waiting for transfers between devices, padded_2(): lax.ppermute(head, axis, [((i + 1) % count, i) for i in range(ends)])  18.1 us
    reduce_sum x5, other arithmetic, products(): jnp.sum(residual * applied)  11.2 us
  transfers between devices with their start and end apart: 32, of which 14 were waited for; matrix products, arithmetic and copies ran while one was open for 0% of the time, Pallas kernels for 0%

commit v1 on v0

--- a/solution.py
+++ b/solution.py
@@ -1,11 +1,21 @@
+import functools
 import jax
 import jax.numpy as jnp
 from jax import lax
 from jax.sharding import PartitionSpec as P
+from jax.lax import psum
 
 ITERS = 3
 discount_rate = 0.05
 diffusion = 0.25
+
+
+def draw_regions(base_x, along_axis, row_axis):
+    r1 = psum(base_x, along_axis)
+    return psum(r1, row_axis)
+
+
+_measure_heads = functools.partial(draw_regions, along_axis="col", row_axis="row")
 
 
 def padded_2(cells, sides, width):
@@ -57,7 +67,7 @@
 
 
 def products(residual, applied):
-    return lax.psum((jnp.sum(residual * residual), jnp.sum(residual * applied)), ("row", "col"))
+    return _measure_heads((jnp.sum(residual * residual), jnp.sum(residual * applied)))
 
 
 def conjugate(coeffs, forcing):

time: 413 us -> 342 us (0.83)
  blocking collectives: 264 us -> 196 us
    psum x6 -> x13, blocking collectives: 264 us -> 196 us  [the longest x6 86.1 us: draw_regions(): return psum(r1, row_axis)]
  transfers between devices with their start and end apart: 32 -> 32, of which waited for: 14 -> 12; matrix products, arithmetic and copies ran while one was open for 0% -> 1% of each run, Pallas kernels for 0% -> 0%
where the time goes in v1:
time: 342 us; the launch traced here: 340 us
  blocking collectives  196 us (57%)
  starting transfers between devices  78.7 us (23%)
  between operations  23.2 us (7%)
  other arithmetic  21.9 us (6%)
  waiting for transfers between devices  20.2 us (6%)
    psum x6, blocking collectives, draw_regions(): return psum(r1, row_axis)  86.1 us
    psum x6, blocking collectives, draw_regions(): r1 = psum(base_x, along_axis)  70 us
    ppermute x16, starting transfers between devices, padded_2(): lax.ppermute(tail, axis, [(i, (i + 1) % count) for i in range(ends)])  57.9 us
    psum x1, blocking collectives, body(): totals = lax.psum((weighted, weight_total), ('row', 'col'))  39.9 us
    ppermute x16, starting transfers between devices, padded_2(): lax.ppermute(head, axis, [((i + 1) % count, i) for i in range(ends)])  20.8 us
    ppermute x16, waiting for transfers between devices, padded_2(): lax.ppermute(head, axis, [((i + 1) % count, i) for i in range(ends)])  15.6 us
    reduce_sum x5, other arithmetic, products(): jnp.sum(residual * applied)  12.1 us
  transfers between devices with their start and end apart: 32, of which 12 were waited for; matrix products, arithmetic and copies ran while one was open for 1% of the time, Pallas kernels for 0%

profile of v1, /device:TPU:0, one launch (start us, length us, event | category | flops | bytes accessed | tf_op | source)
XLA Modules:
  0.0 340.5 jit_solution(263929621522827390)
XLA Ops:
  0.6 1.5 broadcast_add_fusion
  2.2 2.4 collective-permute-start.5
  5.9 5.2 %collective-permute-start.1 = (f32[1,512]{1,0:T(1,128)S(1)}, f32[1,512]{1,0:T(1,128)S(1)}, u32[]{:S(2)}, u32[]{:S(2)}) collective-permute-start(f32[1,512]{1,0:T(1,128)S(1)} %get-tuple-element.77), channel_id=1, source_target_pairs={{0,4},{4,8},{8,12},{12,16},{16,20},{20,24},{24,28},{1,5},{5,9},{9,... | collective-permute-start | bytes 6152 | tf_op jit(solution)/shard_map/ppermute | solution.py:29
  13.8 4.6 %collective-permute-start.7 = (f32[258,1]{1,0:T(8,128)S(1)}, f32[258,1]{1,0:T(8,128)S(1)}, u32[]{:S(2)}, u32[]{:S(2)}) collective-permute-start(f32[258,1]{1,0:T(8,128)S(1)} %get-tuple-element.64), channel_id=1, source_target_pairs={{0,1},{1,2},{2,3},{4,5},{5,6},{6,7},{8,9},{9,10},{10,11},{12,13},{... | collective-permute-start | bytes 3104 | tf_op jit(solution)/shard_map/ppermute | solution.py:29
  19.9 4.9 %collective-permute-start.3 = (f32[258,1]{1,0:T(8,128)S(1)}, f32[258,1]{1,0:T(8,128)S(1)}, u32[]{:S(2)}, u32[]{:S(2)}) collective-permute-start(f32[258,1]{1,0:T(8,128)S(1)} %get-tuple-element.62), channel_id=1, source_target_pairs={{0,1},{1,2},{2,3},{4,5},{5,6},{6,7},{8,9},{9,10},{10,11},{12,13},{... | collective-permute-start | bytes 3104 | tf_op jit(solution)/shard_map/ppermute | solution.py:29
  24.8 2.5 collective-permute-done.2
  27.9 1.4 multiply_reduce_fusion.9
  29.3 12.4 %all-reduce.12 = (f32[]{:T(128)}, f32[]{:T(128)}) all-reduce(f32[]{:T(128)} %get-tuple-element.12, f32[]{:T(128)} %get-tuple-element.11), channel_id=1, replica_groups=mesh['row'=8,'col'=4] {'col'}, use_global_device_ids=true, to_apply=%region_1.0 | all-reduce | flops 2 | bytes 16 | tf_op jit(solution)/shard_map/psum | solution.py:14
  41.7 14.9 %all-reduce.6 = (f32[]{:T(128)}, f32[]{:T(128)}) all-reduce(f32[]{:T(128)} %get-tuple-element.37, f32[]{:T(128)} %get-tuple-element.38), channel_id=1, replica_groups=mesh['row'=8,'col'=4] {'row'}, use_global_device_ids=true, to_apply=%region_2.0 | all-reduce | flops 2 | bytes 16 | tf_op jit(solution)/shard_map/psum | solution.py:15
  58.1 2.2 collective-permute-start.9
  61.6 1.7 collective-permute-done.8
  64.8 4.6 %collective-permute-start.11 = (f32[258,1]{1,0:T(8,128)S(1)}, f32[258,1]{1,0:T(8,128)S(1)}, u32[]{:S(2)}, u32[]{:S(2)}) collective-permute-start(f32[258,1]{1,0:T(8,128)S(1)} %get-tuple-element.60), channel_id=1, source_target_pairs={{0,1},{1,2},{2,3},{4,5},{5,6},{6,7},{8,9},{9,10},{10,11},{12,13},{... | collective-permute-start | bytes 3104 | tf_op jit(solution)/shard_map/ppermute | solution.py:29
  69.4 1.4 collective-permute-done.10
  70.8 1.7 collective-permute-done.11
  72.5 1.4 multiply_reduce_fusion.7
  74.0 12.2 %all-reduce.11 = (f32[]{:T(128)}, f32[]{:T(128)}) all-reduce(f32[]{:T(128)} %get-tuple-element.10, f32[]{:T(128)} %get-tuple-element.9), channel_id=1, replica_groups=mesh['row'=8,'col'=4] {'col'}, use_global_device_ids=true, to_apply=%region_7.0 | all-reduce | flops 2 | bytes 16 | tf_op jit(solution)/shard_map/psum | solution.py:14
  86.2 14.2 %all-reduce.5 = (f32[]{:T(128)}, f32[]{:T(128)}) all-reduce(f32[]{:T(128)} %get-tuple-element.35, f32[]{:T(128)} %get-tuple-element.36), channel_id=1, replica_groups=mesh['row'=8,'col'=4] {'row'}, use_global_device_ids=true, to_apply=%region_8.0 | all-reduce | flops 2 | bytes 16 | tf_op jit(solution)/shard_map/psum | solution.py:15
  105.7 1.9 collective-permute-start.13
  109.0 1.7 collective-permute-done.12
  112.1 4.6 %collective-permute-start.15 = (f32[258,1]{1,0:T(8,128)S(1)}, f32[258,1]{1,0:T(8,128)S(1)}, u32[]{:S(2)}, u32[]{:S(2)}) collective-permute-start(f32[258,1]{1,0:T(8,128)S(1)} %get-tuple-element.58), channel_id=1, source_target_pairs={{0,1},{1,2},{2,3},{4,5},{5,6},{6,7},{8,9},{9,10},{10,11},{12,13},{... | collective-permute-start | bytes 3104 | tf_op jit(solution)/shard_map/ppermute | solution.py:29
  116.7 3.2 collective-permute-start.21
  121.3 1.4 fusion.41
  122.7 10.3 %all-reduce.10 = (f32[]{:T(128)}, f32[]{:T(128)}) all-reduce(f32[]{:T(128)} %get-tuple-element.43, f32[]{:T(128)} %fusion.41), channel_id=1, replica_groups=mesh['row'=8,'col'=4] {'col'}, use_global_device_ids=true, to_apply=%region_13.0 | all-reduce | flops 2 | bytes 16 | tf_op jit(solution)/shard_map/psum | solution.py:14
  133.0 14.2 %all-reduce.4 = (f32[]{:T(128)}, f32[]{:T(128)}) all-reduce(f32[]{:T(128)} %get-tuple-element.33, f32[]{:T(128)} %get-tuple-element.34), channel_id=1, replica_groups=mesh['row'=8,'col'=4] {'row'}, use_global_device_ids=true, to_apply=%region_14.0 | all-reduce | flops 2 | bytes 16 | tf_op jit(solution)/shard_map/psum | solution.py:15
  151.3 1.8 collective-permute-start.17
  156.3 4.6 %collective-permute-start.23 = (f32[258,1]{1,0:T(8,128)S(1)}, f32[258,1]{1,0:T(8,128)S(1)}, u32[]{:S(2)}, u32[]{:S(2)}) collective-permute-start(f32[258,1]{1,0:T(8,128)S(1)} %get-tuple-element.56), channel_id=1, source_target_pairs={{0,1},{1,2},{2,3},{4,5},{5,6},{6,7},{8,9},{9,10},{10,11},{12,13},{... | collective-permute-start | bytes 3104 | tf_op jit(solution)/shard_map/ppermute | solution.py:29
  162.3 4.7 %collective-permute-start.19 = (f32[258,1]{1,0:T(8,128)S(1)}, f32[258,1]{1,0:T(8,128)S(1)}, u32[]{:S(2)}, u32[]{:S(2)}) collective-permute-start(f32[258,1]{1,0:T(8,128)S(1)} %get-tuple-element.54), channel_id=1, source_target_pairs={{0,1},{1,2},{2,3},{4,5},{5,6},{6,7},{8,9},{9,10},{10,11},{12,13},{... | collective-permute-start | bytes 3104 | tf_op jit(solution)/shard_map/ppermute | solution.py:29
  167.1 3.1 collective-permute-done.18
  170.6 3.4 fusion.71
  174.0 12.4 %all-reduce.9 = (f32[]{:T(128)}, f32[]{:T(128)}) all-reduce(f32[]{:T(128)} %get-tuple-element.5, f32[]{:T(128)} %get-tuple-element.4), channel_id=1, replica_groups=mesh['row'=8,'col'=4] {'col'}, use_global_device_ids=true, to_apply=%region_19.0 | all-reduce | flops 2 | bytes 16 | tf_op jit(solution)/shard_map/psum | solution.py:14
  186.4 14.3 %all-reduce.3 = (f32[]{:T(128)}, f32[]{:T(128)}) all-reduce(f32[]{:T(128)} %get-tuple-element.31, f32[]{:T(128)} %get-tuple-element.32), channel_id=1, replica_groups=mesh['row'=8,'col'=4] {'row'}, use_global_device_ids=true, to_apply=%region_20.0 | all-reduce | flops 2 | bytes 16 | tf_op jit(solution)/shard_map/psum | solution.py:15
  202.1 1.8 collective-permute-start.25
  205.2 1.7 collective-permute-done.24
  208.4 4.6 %collective-permute-start.27 = (f32[258,1]{1,0:T(8,128)S(1)}, f32[258,1]{1,0:T(8,128)S(1)}, u32[]{:S(2)}, u32[]{:S(2)}) collective-permute-start(f32[258,1]{1,0:T(8,128)S(1)} %get-tuple-element.52), channel_id=1, source_target_pairs={{0,1},{1,2},{2,3},{4,5},{5,6},{6,7},{8,9},{9,10},{10,11},{12,13},{... | collective-permute-start | bytes 3104 | tf_op jit(solution)/shard_map/ppermute | solution.py:29
  212.9 1.6 collective-permute-done.26
  214.5 1.7 collective-permute-done.27
  216.3 3.9 %multiply_reduce_fusion.2 = (f32[]{:T(128)}, f32[]{:T(128)}, f32[256,512]{1,0:T(8,128)}) fusion(f32[256,512]{1,0:T(8,128)S(1)} %multiply_subtract_fusion.1, f32[1,512]{1,0:T(1,128)S(1)} %collective-permute-done.24, f32[1,512]{1,0:T(1,128)S(1)} %collective-permute-done.25, f32[258,1]{1,0:T(8,128)S(1)} %collective-permute-done.27, ...), kind=kLoop, calls=%fused_computation.138 | loop fusion | flops 7602174 | bytes 2115640 | tf_op jit(solution)/shard_map/reduce_sum | solution.py:70
  220.2 11.2 %all-reduce.8 = (f32[]{:T(128)}, f32[]{:T(128)}) all-reduce(f32[]{:T(128)} %get-tuple-element.8, f32[]{:T(128)} %get-tuple-element.7), channel_id=1, replica_groups=mesh['row'=8,'col'=4] {'col'}, use_global_device_ids=true, to_apply=%region_25.0 | all-reduce | flops 2 | bytes 16 | tf_op jit(solution)/shard_map/psum | solution.py:14
  231.4 14.3 %all-reduce.2 = (f32[]{:T(128)}, f32[]{:T(128)}) all-reduce(f32[]{:T(128)} %get-tuple-element.29, f32[]{:T(128)} %get-tuple-element.30), channel_id=1, replica_groups=mesh['row'=8,'col'=4] {'row'}, use_global_device_ids=true, to_apply=%region_26.0 | all-reduce | flops 2 | bytes 16 | tf_op jit(solution)/shard_map/psum | solution.py:15
  250.2 1.8 multiply_reduce_fusion.1
  252.0 1.8 collective-permute-start.29
  253.8 1.4 collective-permute-start.28
  255.2 1.7 collective-permute-done.28
  258.4 5.2 %collective-permute-start.31 = (f32[258,1]{1,0:T(8,128)S(1)}, f32[258,1]{1,0:T(8,128)}, u32[]{:S(2)}, u32[]{:S(2)}) collective-permute-start(f32[258,1]{1,0:T(8,128)S(1)} %get-tuple-element.50), channel_id=1, source_target_pairs={{0,1},{1,2},{2,3},{4,5},{5,6},{6,7},{8,9},{9,10},{10,11},{12,13},{... | collective-permute-start | bytes 3104 | tf_op jit(solution)/shard_map/ppermute | solution.py:29
  263.6 39.9 %all-reduce = (f32[]{:T(128)}, f32[]{:T(128)}) all-reduce(f32[]{:T(128)} %get-tuple-element.6, f32[]{:T(128)} %get-tuple-element.3), channel_id=1, replica_groups=mesh['row'=8,'col'=4] {'row','col'}, use_global_device_ids=true, to_apply=%region_37.0 | all-reduce | flops 2 | bytes 16 | tf_op jit(solution)/shard_map/psum | solution.py:111
  304.9 4.0 %fusion.5 = f32[]{:T(128)} fusion(f32[256,512]{1,0:T(8,128)S(1)} %get-tuple-element.40, f32[258,1]{1,0:T(8,128)} %collective-permute-done.31, f32[1,512]{1,0:T(1,128)S(1)} %collective-permute-done.28, f32[1,512]{1,0:T(1,128)S(1)} %collective-permute-done.29, f32[258,1]{1,0:T(8,128)} %collective-permute-done.30, f32[256,512]{1,0:T(8,128)S(1)} %get-tuple-element.47, ...), kind=kLoop, calls=%fused_computation.6 | loop fusion | flops 7340031 | bytes 1591348 | tf_op jit(solution)/shard_map/reduce_sum | solution.py:70
  308.9 11.4 %all-reduce.7 = (f32[]{:T(128)}, f32[]{:T(128)}) all-reduce(f32[]{:T(128)} %get-tuple-element.39, f32[]{:T(128)} %fusion.5), channel_id=1, replica_groups=mesh['row'=8,'col'=4] {'col'}, use_global_device_ids=true, to_apply=%region_31.0 | all-reduce | flops 2 | bytes 16 | tf_op jit(solution)/shard_map/psum | solution.py:14
  320.3 14.2 %all-reduce.1 = (f32[]{:T(128)}, f32[]{:T(128)}) all-reduce(f32[]{:T(128)} %get-tuple-element.27, f32[]{:T(128)} %get-tuple-element.28), channel_id=1, replica_groups=mesh['row'=8,'col'=4] {'row'}, use_global_device_ids=true, to_apply=%region_32.0 | all-reduce | flops 2 | bytes 16 | tf_op jit(solution)/shard_map/psum | solution.py:15
  (88 shorter events, 24.0 us)
Async XLA Ops:
  2.2 10.2 %collective-permute-start.5 = (f32[1,512]{1,0:T(1,128)S(1)}, f32[1,512]{1,0:T(1,128)S(1)}, u32[]{:S(2)}, u32[]{:S(2)}) collective-permute-start(f32[1,512]{1,0:T(1,128)S(1)} %get-tuple-element.79), channel_id=1, source_target_pairs={{0,4},{4,8},{8,12},{12,16},{16,20},{20,24},{24,28},{1,5},{5,9},{9,... | collective-permute-start | bytes 6152 | tf_op jit(solution)/shard_map/ppermute | solution.py:29
  4.6 7.8 %collective-permute-start.4 = (f32[1,512]{1,0:T(1,128)S(1)}, f32[1,512]{1,0:T(1,128)S(1)}, u32[]{:S(2)}, u32[]{:S(2)}) collective-permute-start(f32[1,512]{1,0:T(1,128)S(1)} %get-tuple-element.80), channel_id=1, source_target_pairs={{4,0},{8,4},{12,8},{16,12},{20,16},{24,20},{28,24},{5,1},{9,5},{13... | collective-permute-start | bytes 6152 | tf_op jit(solution)/shard_map/ppermute | solution.py:31
  5.9 12.5 %collective-permute-start.1 = (f32[1,512]{1,0:T(1,128)S(1)}, f32[1,512]{1,0:T(1,128)S(1)}, u32[]{:S(2)}, u32[]{:S(2)}) collective-permute-start(f32[1,512]{1,0:T(1,128)S(1)} %get-tuple-element.77), channel_id=1, source_target_pairs={{0,4},{4,8},{8,12},{12,16},{16,20},{20,24},{24,28},{1,5},{5,9},{9,... | collective-permute-start | bytes 6152 | tf_op jit(solution)/shard_map/ppermute | solution.py:29
  11.1 7.3 %collective-permute-start = (f32[1,512]{1,0:T(1,128)S(1)}, f32[1,512]{1,0:T(1,128)S(1)}, u32[]{:S(2)}, u32[]{:S(2)}) collective-permute-start(f32[1,512]{1,0:T(1,128)S(1)} %get-tuple-element.78), channel_id=1, source_target_pairs={{4,0},{8,4},{12,8},{16,12},{20,16},{24,20},{28,24},{5,1},{9,5},{13... | collective-permute-start | bytes 6152 | tf_op jit(solution)/shard_map/ppermute | solution.py:31
  12.5 12.2 %collective-permute-start.6 = (f32[258,1]{1,0:T(8,128)S(1)}, f32[258,1]{1,0:T(8,128)S(1)}, u32[]{:S(2)}, u32[]{:S(2)}) collective-permute-start(f32[258,1]{1,0:T(8,128)S(1)} %get-tuple-element.63), channel_id=1, source_target_pairs={{1,0},{2,1},{3,2},{5,4},{6,5},{7,6},{9,8},{10,9},{11,10},{13,12},{... | collective-permute-start | bytes 3104 | tf_op jit(solution)/shard_map/ppermute | solution.py:31
  13.8 11.0 %collective-permute-start.7 = (f32[258,1]{1,0:T(8,128)S(1)}, f32[258,1]{1,0:T(8,128)S(1)}, u32[]{:S(2)}, u32[]{:S(2)}) collective-permute-start(f32[258,1]{1,0:T(8,128)S(1)} %get-tuple-element.64), channel_id=1, source_target_pairs={{0,1},{1,2},{2,3},{4,5},{5,6},{6,7},{8,9},{9,10},{10,11},{12,13},{... | collective-permute-start | bytes 3104 | tf_op jit(solution)/shard_map/ppermute | solution.py:29
  18.4 102.8 %copy-start.4 = (f32[1,512]{1,0:T(1,128)}, f32[1,512]{1,0:T(1,128)S(1)}, u32[]{:S(2)}) copy-start(f32[1,512]{1,0:T(1,128)S(1)} %collective-permute-done) | copy-start | bytes 6148
  18.6 8.7 %collective-permute-start.2 = (f32[258,1]{1,0:T(8,128)S(1)}, f32[258,1]{1,0:T(8,128)S(1)}, u32[]{:S(2)}, u32[]{:S(2)}) collective-permute-start(f32[258,1]{1,0:T(8,128)S(1)} %get-tuple-element.61), channel_id=1, source_target_pairs={{1,0},{2,1},{3,2},{5,4},{6,5},{7,6},{9,8},{10,9},{11,10},{13,12},{... | collective-permute-start | bytes 3104 | tf_op jit(solution)/shard_map/ppermute | solution.py:31
  19.9 8.0 %collective-permute-start.3 = (f32[258,1]{1,0:T(8,128)S(1)}, f32[258,1]{1,0:T(8,128)S(1)}, u32[]{:S(2)}, u32[]{:S(2)}) collective-permute-start(f32[258,1]{1,0:T(8,128)S(1)} %get-tuple-element.62), channel_id=1, source_target_pairs={{0,1},{1,2},{2,3},{4,5},{5,6},{6,7},{8,9},{9,10},{10,11},{12,13},{... | collective-permute-start | bytes 3104 | tf_op jit(solution)/shard_map/ppermute | solution.py:29
  58.1 3.6 %collective-permute-start.9 = (f32[1,512]{1,0:T(1,128)S(1)}, f32[1,512]{1,0:T(1,128)S(1)}, u32[]{:S(2)}, u32[]{:S(2)}) collective-permute-start(f32[1,512]{1,0:T(1,128)S(1)} %get-tuple-element.75), channel_id=1, source_target_pairs={{0,4},{4,8},{8,12},{12,16},{16,20},{20,24},{24,28},{1,5},{5,9},{9,... | collective-permute-start | bytes 6152 | tf_op jit(solution)/shard_map/ppermute | solution.py:29
  60.3 3.1 collective-permute-start.8
  63.5 7.3 %collective-permute-start.10 = (f32[258,1]{1,0:T(8,128)S(1)}, f32[258,1]{1,0:T(8,128)S(1)}, u32[]{:S(2)}, u32[]{:S(2)}) collective-permute-start(f32[258,1]{1,0:T(8,128)S(1)} %get-tuple-element.59), channel_id=1, source_target_pairs={{1,0},{2,1},{3,2},{5,4},{6,5},{7,6},{9,8},{10,9},{11,10},{13,12},{... | collective-permute-start | bytes 3104 | tf_op jit(solution)/shard_map/ppermute | solution.py:31
  64.8 7.8 %collective-permute-start.11 = (f32[258,1]{1,0:T(8,128)S(1)}, f32[258,1]{1,0:T(8,128)S(1)}, u32[]{:S(2)}, u32[]{:S(2)}) collective-permute-start(f32[258,1]{1,0:T(8,128)S(1)} %get-tuple-element.60), channel_id=1, source_target_pairs={{0,1},{1,2},{2,3},{4,5},{5,6},{6,7},{8,9},{9,10},{10,11},{12,13},{... | collective-permute-start | bytes 3104 | tf_op jit(solution)/shard_map/ppermute | solution.py:29
  105.7 11.0 %copy-start.1 = (f32[256,512]{1,0:T(8,128)S(1)}, f32[256,512]{1,0:T(8,128)}, u32[]{:S(2)}) copy-start(f32[256,512]{1,0:T(8,128)} %param.7) | copy-start | bytes 1572868
  105.7 3.2 collective-permute-start.13
  107.7 3.1 collective-permute-start.12
  110.8 10.4 %collective-permute-start.14 = (f32[258,1]{1,0:T(8,128)S(1)}, f32[258,1]{1,0:T(8,128)S(1)}, u32[]{:S(2)}, u32[]{:S(2)}) collective-permute-start(f32[258,1]{1,0:T(8,128)S(1)} %get-tuple-element.57), channel_id=1, source_target_pairs={{1,0},{2,1},{3,2},{5,4},{6,5},{7,6},{9,8},{10,9},{11,10},{13,12},{... | collective-permute-start | bytes 3104 | tf_op jit(solution)/shard_map/ppermute | solution.py:31
  112.1 9.1 %collective-permute-start.15 = (f32[258,1]{1,0:T(8,128)S(1)}, f32[258,1]{1,0:T(8,128)S(1)}, u32[]{:S(2)}, u32[]{:S(2)}) collective-permute-start(f32[258,1]{1,0:T(8,128)S(1)} %get-tuple-element.58), channel_id=1, source_target_pairs={{0,1},{1,2},{2,3},{4,5},{5,6},{6,7},{8,9},{9,10},{10,11},{12,13},{... | collective-permute-start | bytes 3104 | tf_op jit(solution)/shard_map/ppermute | solution.py:29
  116.7 37.6 %collective-permute-start.21 = (f32[1,512]{1,0:T(1,128)S(1)}, f32[1,512]{1,0:T(1,128)S(1)}, u32[]{:S(2)}, u32[]{:S(2)}) collective-permute-start(f32[1,512]{1,0:T(1,128)S(1)} %get-tuple-element.71), channel_id=1, source_target_pairs={{0,4},{4,8},{8,12},{12,16},{16,20},{20,24},{24,28},{1,5},{5,9},{9,... | collective-permute-start | bytes 6152 | tf_op jit(solution)/shard_map/ppermute | solution.py:29
  119.9 34.4 %collective-permute-start.20 = (f32[1,512]{1,0:T(1,128)S(1)}, f32[1,512]{1,0:T(1,128)S(1)}, u32[]{:S(2)}, u32[]{:S(2)}) collective-permute-start(f32[1,512]{1,0:T(1,128)S(1)} %get-tuple-element.72), channel_id=1, source_target_pairs={{4,0},{8,4},{12,8},{16,12},{20,16},{24,20},{28,24},{5,1},{9,5},{13... | collective-permute-start | bytes 6152 | tf_op jit(solution)/shard_map/ppermute | solution.py:31
  151.3 153.6 %copy-start = (f32[256,512]{1,0:T(8,128)}, f32[256,512]{1,0:T(8,128)S(1)}, u32[]{:S(2)}) copy-start(f32[256,512]{1,0:T(8,128)S(1)} %multiply_add_fusion.1) | copy-start | bytes 1572868
  151.3 9.5 %collective-permute-start.17 = (f32[1,512]{1,0:T(1,128)S(1)}, f32[1,512]{1,0:T(1,128)S(1)}, u32[]{:S(2)}, u32[]{:S(2)}) collective-permute-start(f32[1,512]{1,0:T(1,128)S(1)} %get-tuple-element.69), channel_id=1, source_target_pairs={{0,4},{4,8},{8,12},{12,16},{16,20},{20,24},{24,28},{1,5},{5,9},{9,... | collective-permute-start | bytes 6152 | tf_op jit(solution)/shard_map/ppermute | solution.py:29
  153.1 7.8 %collective-permute-start.16 = (f32[1,512]{1,0:T(1,128)S(1)}, f32[1,512]{1,0:T(1,128)S(1)}, u32[]{:S(2)}, u32[]{:S(2)}) collective-permute-start(f32[1,512]{1,0:T(1,128)S(1)} %get-tuple-element.70), channel_id=1, source_target_pairs={{4,0},{8,4},{12,8},{16,12},{20,16},{24,20},{28,24},{5,1},{9,5},{13... | collective-permute-start | bytes 6152 | tf_op jit(solution)/shard_map/ppermute | solution.py:31
  154.4 0.6 copy-start.11
  154.4 0.6 copy-start.13
  155.0 12.1 %collective-permute-start.22 = (f32[258,1]{1,0:T(8,128)S(1)}, f32[258,1]{1,0:T(8,128)S(1)}, u32[]{:S(2)}, u32[]{:S(2)}) collective-permute-start(f32[258,1]{1,0:T(8,128)S(1)} %get-tuple-element.55), channel_id=1, source_target_pairs={{1,0},{2,1},{3,2},{5,4},{6,5},{7,6},{9,8},{10,9},{11,10},{13,12},{... | collective-permute-start | bytes 3104 | tf_op jit(solution)/shard_map/ppermute | solution.py:31
  156.3 10.8 %collective-permute-start.23 = (f32[258,1]{1,0:T(8,128)S(1)}, f32[258,1]{1,0:T(8,128)S(1)}, u32[]{:S(2)}, u32[]{:S(2)}) collective-permute-start(f32[258,1]{1,0:T(8,128)S(1)} %get-tuple-element.56), channel_id=1, source_target_pairs={{0,1},{1,2},{2,3},{4,5},{5,6},{6,7},{8,9},{9,10},{10,11},{12,13},{... | collective-permute-start | bytes 3104 | tf_op jit(solution)/shard_map/ppermute | solution.py:29
  160.8 55.4 %copy-start.7 = (f32[1,512]{1,0:T(1,128)}, f32[1,512]{1,0:T(1,128)S(1)}, u32[]{:S(2)}) copy-start(f32[1,512]{1,0:T(1,128)S(1)} %collective-permute-done.17) | copy-start | bytes 6148
  160.9 55.4 %copy-start.9 = (f32[1,512]{1,0:T(1,128)}, f32[1,512]{1,0:T(1,128)S(1)}, u32[]{:S(2)}) copy-start(f32[1,512]{1,0:T(1,128)S(1)} %collective-permute-done.16) | copy-start | bytes 6148
  160.9 9.7 %copy-start.12 = (f32[1,512]{1,0:T(1,128)S(1)}, f32[1,512]{1,0:T(1,128)}, u32[]{:S(2)}) copy-start(f32[1,512]{1,0:T(1,128)} %copy-done.11) | copy-start | bytes 6148
  160.9 9.7 %copy-start.14 = (f32[1,512]{1,0:T(1,128)S(1)}, f32[1,512]{1,0:T(1,128)}, u32[]{:S(2)}) copy-start(f32[1,512]{1,0:T(1,128)} %copy-done.13) | copy-start | bytes 6148
  161.0 9.6 %copy-start.5 = (f32[1,512]{1,0:T(1,128)S(1)}, f32[1,512]{1,0:T(1,128)}, u32[]{:S(2)}) copy-start(f32[1,512]{1,0:T(1,128)} %copy-done.4) | copy-start | bytes 6148
  161.0 9.2 %collective-permute-start.18 = (f32[258,1]{1,0:T(8,128)S(1)}, f32[258,1]{1,0:T(8,128)S(1)}, u32[]{:S(2)}, u32[]{:S(2)}) collective-permute-start(f32[258,1]{1,0:T(8,128)S(1)} %get-tuple-element.53), channel_id=1, source_target_pairs={{1,0},{2,1},{3,2},{5,4},{6,5},{7,6},{9,8},{10,9},{11,10},{13,12},{... | collective-permute-start | bytes 3104 | tf_op jit(solution)/shard_map/ppermute | solution.py:31
  162.3 8.3 %collective-permute-start.19 = (f32[258,1]{1,0:T(8,128)S(1)}, f32[258,1]{1,0:T(8,128)S(1)}, u32[]{:S(2)}, u32[]{:S(2)}) collective-permute-start(f32[258,1]{1,0:T(8,128)S(1)} %get-tuple-element.54), channel_id=1, source_target_pairs={{0,1},{1,2},{2,3},{4,5},{5,6},{6,7},{8,9},{9,10},{10,11},{12,13},{... | collective-permute-start | bytes 3104 | tf_op jit(solution)/shard_map/ppermute | solution.py:29
  170.6 45.7 %copy-start.2 = (f32[258,1]{1,0:T(8,128)}, f32[258,1]{1,0:T(8,128)S(1)}, u32[]{:S(2)}) copy-start(f32[258,1]{1,0:T(8,128)S(1)} %collective-permute-done.19) | copy-start | bytes 3100
  202.1 3.1 collective-permute-start.25
  203.9 3.1 collective-permute-start.24
  207.1 7.5 %collective-permute-start.26 = (f32[258,1]{1,0:T(8,128)S(1)}, f32[258,1]{1,0:T(8,128)S(1)}, u32[]{:S(2)}, u32[]{:S(2)}) collective-permute-start(f32[258,1]{1,0:T(8,128)S(1)} %get-tuple-element.51), channel_id=1, source_target_pairs={{1,0},{2,1},{3,2},{5,4},{6,5},{7,6},{9,8},{10,9},{11,10},{13,12},{... | collective-permute-start | bytes 3104 | tf_op jit(solution)/shard_map/ppermute | solution.py:31
  208.4 7.9 %collective-permute-start.27 = (f32[258,1]{1,0:T(8,128)S(1)}, f32[258,1]{1,0:T(8,128)S(1)}, u32[]{:S(2)}, u32[]{:S(2)}) collective-permute-start(f32[258,1]{1,0:T(8,128)S(1)} %get-tuple-element.52), channel_id=1, source_target_pairs={{0,1},{1,2},{2,3},{4,5},{5,6},{6,7},{8,9},{9,10},{10,11},{12,13},{... | collective-permute-start | bytes 3104 | tf_op jit(solution)/shard_map/ppermute | solution.py:29
  252.0 3.2 collective-permute-start.29
  253.8 51.1 %copy-start.3 = (f32[258,1]{1,0:T(8,128)S(1)}, f32[258,1]{1,0:T(8,128)}, u32[]{:S(2)}) copy-start(f32[258,1]{1,0:T(8,128)} %copy-done.2) | copy-start | bytes 3100
  253.8 3.2 collective-permute-start.28
  257.0 47.9 %copy-start.10 = (f32[1,512]{1,0:T(1,128)S(1)}, f32[1,512]{1,0:T(1,128)}, u32[]{:S(2)}) copy-start(f32[1,512]{1,0:T(1,128)} %copy-done.9) | copy-start | bytes 6148
  257.1 47.7 %collective-permute-start.30 = (f32[258,1]{1,0:T(8,128)S(1)}, f32[258,1]{1,0:T(8,128)}, u32[]{:S(2)}, u32[]{:S(2)}) collective-permute-start(f32[258,1]{1,0:T(8,128)S(1)} %get-tuple-element.49), channel_id=1, source_target_pairs={{1,0},{2,1},{3,2},{5,4},{6,5},{7,6},{9,8},{10,9},{11,10},{13,12},{... | collective-permute-start | bytes 3104 | tf_op jit(solution)/shard_map/ppermute | solution.py:31
  258.4 46.4 %collective-permute-start.31 = (f32[258,1]{1,0:T(8,128)S(1)}, f32[258,1]{1,0:T(8,128)}, u32[]{:S(2)}, u32[]{:S(2)}) collective-permute-start(f32[258,1]{1,0:T(8,128)S(1)} %get-tuple-element.50), channel_id=1, source_target_pairs={{0,1},{1,2},{2,3},{4,5},{5,6},{6,7},{8,9},{9,10},{10,11},{12,13},{... | collective-permute-start | bytes 3104 | tf_op jit(solution)/shard_map/ppermute | solution.py:29
  303.5 1.4 copy-start.8
  303.5 1.4 copy-start.6
